TPU v7x, 32 devices: a whole 2x2x4 slice. The times are simulated.
32 devices in a mesh: lat: 4 (over z), lon: 8 (over y, x, core).
Axes of the slice: x: 2, y: 2, z: 4, core: 2. Of those that a mesh axis runs over, the one named last changes fastest.
Arguments:
- fields: float32 [5, 960, 2880], P(None, 'lat', 'lon'), may hold values from -6 to 6
- east_courant: float32 [960, 2880], P('lat', 'lon'), may hold values from -0.4 to 0.4
- north_courant: float32 [960, 2880], P('lat', 'lon'), may hold values from -0.4 to 0.4
- cutoff: int32 [960], replicated, may hold values from 1 to 1439
- damping: float32 [960], replicated, may hold values from 0.05 to 0.5
- ship_rows: int32 [4, 4, 60], replicated, may hold values from -1 to 239, as said below
Outputs:
- updated: float32 [5, 960, 2880], P(None, 'lat', 'lon')
Inputs may be any that keep to these rules, and one draw needn't show every extreme that they name: ship_rows[s, d, j] is a row of band s (0 to 239) whose filter is computed by band d, or -1 for an empty slot; no row is listed twice; every row within 240 rows of either pole is listed, no row farther than 360 from both poles is listed, and rows between are listed or not, so that bands 0 and 3 are covered whole; a band's listed rows fill the slots of its destinations in full except the last destination it uses, so band 0 fills 60 slots to some band.
All inputs are finite; a program needn't handle non-finite values.
Results may differ from a plain program's by a relative error of at most 0.0003.
Values sent between devices are 32-bit elements; how exact they have to be, the bound alone decides.
A program may use at most 256 MiB of HBM per device.

v0:
```python
import math
import jax
import jax.numpy as jnp
from jax import lax
from jax.sharding import PartitionSpec as P

HIGHEST_PRECISION = lax.Precision.HIGHEST


def with_halo(cells, sides, width, closed):
    for axis, dim in sides:
        count = lax.axis_size(axis)
        ends = count if closed else count - 1
        head = lax.slice_in_dim(cells, 0, width, axis=dim)
        tail = lax.slice_in_dim(cells, cells.shape[dim] - width, cells.shape[dim], axis=dim)
        cells = jnp.concatenate(
            [
                lax.ppermute(tail, axis, [(i, (i + 1) % count) for i in range(ends)]),
                cells,
                lax.ppermute(head, axis, [((i + 1) % count, i) for i in range(ends)]),
            ],
            axis=dim,
        )
    return cells


def phase_pair(cutoffs, positions, length):
    turned = (2 * cutoffs[:, None] + 1) * positions[None, :] % (2 * length)
    angles = turned.astype(jnp.float32) * (math.pi / length)
    return (jnp.cos(angles), jnp.sin(angles))


def kernel_block(sources, targets, length):
    offsets = targets[None, :] - sources[:, None]
    magnitude = jnp.abs(offsets)
    nearest = jnp.minimum(magnitude, length - magnitude)
    nonzero = jnp.where(nearest == 0, 1, nearest)
    values = jnp.sign(offsets).astype(jnp.float32) / (
        length * jnp.sin(nonzero.astype(jnp.float32) * (math.pi / length))
    )
    return jnp.where(offsets == 0, jnp.float32(0.0), values)


def modulated_sum(running, column_piece, cutoffs, targets, length):
    piece_count = column_piece.shape[2]
    sources = jnp.arange(piece_count, dtype=jnp.int32)
    cos_part, sin_part = phase_pair(cutoffs, sources, length)
    stacked = jnp.stack([column_piece * cos_part[:, None, :], column_piece * sin_part[:, None, :]])
    flattened = stacked.reshape(-1, piece_count)
    kernel = kernel_block(sources, targets, length)
    product = jnp.dot(
        flattened, kernel, precision=HIGHEST_PRECISION, preferred_element_type=jnp.float32
    )
    return product.reshape(running.shape)


def finish_filter(running, local_rows, cutoffs, targets, damping_rows, length):
    cos_part, sin_part = phase_pair(cutoffs, targets, length)
    centre = (2 * cutoffs + 1).astype(jnp.float32) / length
    lowpass = (
        sin_part[:, None, :] * running[0]
        - cos_part[:, None, :] * running[1]
        + centre[:, None, None] * local_rows
    )
    return damping_rows[:, None, None] * local_rows + (1.0 - damping_rows[:, None, None]) * lowpass


def table_lookup(lookup_table, indices):
    matches = indices[:, None] == jnp.arange(lookup_table.shape[0], dtype=jnp.int32)[None, :]
    return jnp.sum(
        jnp.where(matches, lookup_table[None, :], jnp.zeros_like(lookup_table)[None, :]), axis=1
    )


def per_device(fields, east_courant, north_courant, cutoff, damping, ship_rows):
    channel_count, rows_dev, cols_dev = fields.shape
    band_count = lax.axis_size("lat")
    segment_count = lax.axis_size("lon")
    lat_count = rows_dev * band_count
    lon_count = cols_dev * segment_count
    band_index = lax.axis_index("lat")
    segment_index = lax.axis_index("lon")
    zonal = with_halo(jnp.concatenate([fields, east_courant[None]], axis=0), (("lon", 2),), 1, True)
    meridional = with_halo(
        jnp.concatenate([fields, north_courant[None]], axis=0), (("lat", 1),), 1, False
    )
    east_cells = zonal[:channel_count, :, 2:]
    west_cells = zonal[:channel_count, :, :-2]
    west_courant = zonal[channel_count, :, :-2]
    east_flux = east_courant * jnp.where(east_courant > 0, fields, east_cells)
    west_flux = west_courant * jnp.where(west_courant > 0, west_cells, fields)
    global_rows = band_index * rows_dev + jnp.arange(rows_dev, dtype=jnp.int32)
    latitudes = global_rows.astype(jnp.float32)
    face_n = jnp.sin((latitudes + 1.0) * (math.pi / lat_count))
    face_s = jnp.sin(latitudes * (math.pi / lat_count))
    centre = jnp.sin((latitudes + 0.5) * (math.pi / lat_count))
    north_mask = (global_rows < lat_count - 1).astype(jnp.float32)
    south_mask = (global_rows > 0).astype(jnp.float32)
    north_cells = meridional[:channel_count, 2:, :]
    south_cells = meridional[:channel_count, :-2, :]
    south_courant = meridional[channel_count, :-2, :]
    north_flux = (
        north_courant
        * jnp.where(north_courant > 0, fields, north_cells)
        * (face_n * north_mask)[:, None]
    )
    south_flux = (
        south_courant
        * jnp.where(south_courant > 0, south_cells, fields)
        * (face_s * south_mask)[:, None]
    )
    advected = fields - (east_flux - west_flux) - (north_flux - south_flux) / centre[:, None]
    outgoing_rows = lax.dynamic_index_in_dim(ship_rows, band_index, axis=0, keepdims=False).reshape(
        -1
    )
    outgoing_valid = outgoing_rows >= 0
    picked = jnp.take(advected, jnp.maximum(outgoing_rows, 0), axis=1)
    picked = jnp.where(outgoing_valid[None, :, None], picked, jnp.float32(0.0)).transpose(1, 0, 2)
    slot_count = picked.shape[0]
    arrived = lax.all_to_all(
        picked.reshape(band_count, -1, channel_count, cols_dev),
        "lat",
        split_axis=0,
        concat_axis=0,
        tiled=True,
    )
    arrived = arrived.reshape(slot_count, channel_count, cols_dev)
    incoming_rows = lax.dynamic_index_in_dim(ship_rows, band_index, axis=1, keepdims=False).reshape(
        -1
    )
    capacity = slot_count // band_count
    source_band = jnp.arange(slot_count, dtype=jnp.int32) // capacity
    incoming_global = jnp.where(incoming_rows >= 0, source_band * rows_dev + incoming_rows, 0)
    cutoffs = table_lookup(cutoff, incoming_global)
    damping_rows = table_lookup(damping, incoming_global)
    targets = segment_index * cols_dev + jnp.arange(cols_dev, dtype=jnp.int32)
    initial = jnp.zeros((2,) + arrived.shape, jnp.float32)
    running = modulated_sum(
        initial, lax.all_gather(arrived, "lon", axis=2, tiled=True), cutoffs, targets, lon_count
    )
    filtered = finish_filter(running, arrived, cutoffs, targets, damping_rows, lon_count)
    returned = lax.all_to_all(
        filtered.reshape(band_count, -1, channel_count, cols_dev),
        "lat",
        split_axis=0,
        concat_axis=0,
        tiled=True,
    )
    returned = returned.reshape(slot_count, channel_count, cols_dev)
    placement = jnp.where(outgoing_valid, outgoing_rows, rows_dev)
    return advected.at[:, placement, :].set(returned.transpose(1, 0, 2), mode="drop")


def solution(mesh):
    placed = (P(None, "lat", "lon"), P("lat", "lon"), P("lat", "lon"), P(), P(), P())
    return jax.shard_map(
        per_device, mesh=mesh, in_specs=placed, out_specs=P(None, "lat", "lon"), check_vma=False
    )
```

profile of v0, /device:TPU:0, one launch (start us, length us, event | category | flops | bytes accessed | tf_op | source)
XLA Modules:
  0.0 518.8 jit_solution(7479676274369579383)
XLA Ops:
  6.5 2.3 copy.66
  9.8 4.9 collective-permute-start.3
  17.4 2.0 copy.63
  20.7 2.7 collective-permute-start
  32.0 1.8 copy.64
  33.8 1.8 maximum_bitcast_fusion
  35.6 1.7 fusion.52
  37.3 1.9 copy.62
  39.2 4.4 fusion.42
  44.6 5.1 fusion.23
  49.7 2.6 gather_fusion
  54.0 50.3 %all_to_all.10 = f32[4,60,5,360]{3,1,2,0:T(8,128)S(1)} all-to-all(f32[4,60,5,360]{3,1,2,0:T(8,128)S(1)} %copy.69), channel_id=1, replica_groups=mesh['lat'=4,'lon'=8] {'lat'}, dimensions={0} | all-to-all | bytes 3456000 | tf_op jit(solution)/shard_map/all_to_all | solution.py:120
  104.3 3.6 copy.81
  107.9 5.2 %reshape.289 = f32[240,5,360]{0,1,2:T(8,128)} reshape(f32[4,60,5,360]{1,0,2,3:T(4,128)} %copy.81) | data formatting | bytes 3456000 | tf_op jit(solution)/shard_map/reshape | solution.py:127
  114.7 1.7 fusion.50
  116.4 13.7 %fusion.30 = (f32[240,2880]{0,1:T(8,128)}, f32[240,2880]{0,1:T(8,128)}) fusion(s32[240]{0:T(256)S(1)} %multiply_add_fusion), kind=kLoop, calls=%fused_computation.45 | loop fusion | flops 6220800 | bytes 5530560 | tf_op jit(solution)/shard_map/cos | solution.py:30
  130.1 18.3 %fusion.66 = f32[2880,360]{1,0:T(8,128)} fusion(s32[360]{0:T(512)S(1)} %iota_add_fusion), kind=kLoop, calls=%fused_computation.12.clone.clone.1 | loop fusion | flops 14515200 | bytes 4148640 | tf_op jit(solution)/shard_map/dot_general | solution.py:51
  148.4 81.8 %all-gather.2.cloned.1.call-done = f32[240,5,2880]{0,1,2:T(8,128)} async-done(((f32[240,5,360]{0,1,2:T(8,128)}), f32[240,5,2880]{0,1,2:T(8,128)}) %all-gather.2.cloned.1.call-update) | async-done | bytes 13824016 | tf_op jit(solution)/shard_map/all_gather | solution.py:139
  230.1 26.0 %multiply_bitcast_fusion.1 = (f32[1,240,5,2880]{1,2,3,0:T(8,128)}, f32[1,240,5,2880]{1,2,3,0:T(8,128)}) fusion(f32[240,5,2880]{0,1,2:T(8,128)} %all-gather.2.cloned.1.call-done, f32[240,2880]{0,1:T(8,128)} %get-tuple-element.17, f32[240,2880]{0,1:T(8,128)} %get-tuple-element.18), kind=kLoop, calls=%fused_computation.4 | loop fusion | flops 6912000 | bytes 47001600 | tf_op jit(solution)/shard_map/stack | solution.py:48
  256.1 34.0 %pad_maximum_fusion = f32[2,240,5,2880]{1,2,3,0:T(8,128)} fusion(f32[1,240,5,2880]{1,2,3,0:T(8,128)} %get-tuple-element.8, f32[1,240,5,2880]{1,2,3,0:T(8,128)} %get-tuple-element.7), kind=kLoop, calls=%fused_computation.2 | loop fusion | flops 6912000 | bytes 55296000 | tf_op jit(solution)/shard_map/stack | solution.py:48
  290.1 47.7 %copy.73 = f32[2,240,5,2880]{3,2,1,0:T(8,128)} copy(f32[2,240,5,2880]{1,2,3,0:T(8,128)} %pad_maximum_fusion) | data formatting | bytes 55296000 | tf_op jit(solution)/shard_map/stack | solution.py:48
  337.8 35.2 %reshape.271 = f32[2400,2880]{1,0:T(8,128)} reshape(f32[2,240,5,2880]{3,2,1,0:T(8,128)} %copy.73) | data formatting | bytes 55296000 | tf_op jit(solution)/shard_map/reshape | solution.py:49
  373.0 43.7 %fusion.6 = f32[2400,360]{0,1:T(8,128)S(1)} fusion(f32[2400,2880]{1,0:T(8,128)} %reshape.271, f32[2880,360]{1,0:T(8,128)} %fusion.66), kind=kOutput, calls=%fused_computation.13 | convolution fusion | flops 29859840000 | bytes 35251200 | tf_op jit(solution)/shard_map/dot_general | solution.py:51
  416.7 2.4 fusion.61
  419.2 2.8 copy.75
  422.0 3.1 squeeze.13
  425.1 2.8 copy.74
  427.8 3.1 squeeze.12
  430.9 4.7 fusion.13
  436.0 50.2 %all_to_all.11 = f32[4,60,5,360]{3,1,2,0:T(8,128)S(1)} all-to-all(f32[4,60,5,360]{3,1,2,0:T(8,128)S(1)} %copy.77), channel_id=1, replica_groups=mesh['lat'=4,'lon'=8] {'lat'}, dimensions={0} | all-to-all | bytes 3456000 | tf_op jit(solution)/shard_map/all_to_all | solution.py:142
  486.2 2.7 copy.82
  488.9 21.5 %scatter_fusion = f32[5,240,360]{2,0,1:T(8,128)S(1)} fusion(f32[5,240,360]{2,0,1:T(8,128)S(1)} %copy-done, s32[240]{0:T(256)S(1)} %bitcast.30, f32[240,5,360]{2,1,0:T(8,128)} %bitcast.28), kind=kCustom, calls=%fused_computation.1 | custom fusion | bytes 5184960 | tf_op jit(solution)/shard_map/scatter | solution.py:151
  (70 shorter events, 19.5 us)
Async XLA Ops:
  6.5 223.6 %all-gather.2.cloned.1.call-start = ((), (), s32[]{:S(2)}) async-start(), calls=%async_computation.2 | async-start | bytes 26542080 | tf_op jit(solution)/shard_map/all_gather | solution.py:139
  6.5 2.3 copy-start.5
  8.9 7.2 %copy-start.1 = (f32[5,240,360]{2,1,0:T(8,128)S(1)}, f32[5,240,360]{2,1,0:T(8,128)}, u32[]{:S(2)}) copy-start(f32[5,240,360]{2,1,0:T(8,128)} %param.6) | copy-start | bytes 5184004
  8.9 7.2 %copy-start.2 = (f32[240,360]{1,0:T(8,128)S(1)}, f32[240,360]{1,0:T(8,128)}, u32[]{:S(2)}) copy-start(f32[240,360]{1,0:T(8,128)} %param.7) | copy-start | bytes 1036804
  9.1 8.2 %copy-start.3 = (f32[1,240,360]{2,0,1:T(1,128)}, f32[1,240,360]{2,0,1:T(1,128)S(1)}, u32[]{:S(2)}) copy-start(f32[1,240,360]{2,0,1:T(1,128)S(1)} %broadcast_in_dim.115) | copy-start | bytes 1036804
  9.8 33.8 %collective-permute-start.3 = (f32[6,1,360]{2,0,1:T(8,128)}, f32[6,1,360]{2,0,1:T(8,128)S(1)}, u32[]{:S(2)}, u32[]{:S(2)}) collective-permute-start(f32[6,1,360]{2,0,1:T(8,128)} %get-tuple-element.12), channel_id=1, source_target_pairs={{0,8},{8,16},{16,24},{1,9},{9,17},{17,25},{2,10},{10,18},{18,26},{... | collective-permute-start | bytes 25928 | tf_op jit(solution)/shard_map/ppermute | solution.py:18
  14.7 29.7 %collective-permute-start.2 = (f32[6,1,360]{2,0,1:T(8,128)S(1)}, f32[6,1,360]{2,0,1:T(8,128)S(1)}, u32[]{:S(2)}, u32[]{:S(2)}) collective-permute-start(f32[6,1,360]{2,0,1:T(8,128)S(1)} %get-tuple-element.11), channel_id=1, source_target_pairs={{8,0},{16,8},{24,16},{9,1},{17,9},{25,17},{10,2},{18,10},{26,18},{... | collective-permute-start | bytes 25928 | tf_op jit(solution)/shard_map/ppermute | solution.py:20
  19.4 12.6 %collective-permute-start.1 = (f32[6,240,1]{1,2,0:T(1,128)}, f32[6,240,1]{1,2,0:T(1,128)}, u32[]{:S(2)}, u32[]{:S(2)}) collective-permute-start(f32[6,240,1]{1,2,0:T(1,128)} %copy.63), channel_id=1, source_target_pairs={{0,1},{1,2},{2,3},{3,4},{4,5},{5,6},{6,7},{7,0},{8,9},{9,10},{10,1... | collective-permute-start | bytes 17288 | tf_op jit(solution)/shard_map/ppermute | solution.py:18
  20.7 16.6 %collective-permute-start = (f32[6,240,1]{1,2,0:T(1,128)S(1)}, f32[6,240,1]{1,2,0:T(1,128)}, u32[]{:S(2)}, u32[]{:S(2)}) collective-permute-start(f32[6,240,1]{1,2,0:T(1,128)S(1)} %copy.61), channel_id=1, source_target_pairs={{1,0},{2,1},{3,2},{4,3},{5,4},{6,5},{7,6},{0,7},{9,8},{10,9},{11,1... | collective-permute-start | bytes 17288 | tf_op jit(solution)/shard_map/ppermute | solution.py:20
  39.2 4.4 copy-start.4
  43.6 1.0 copy-start.6
  43.6 1.0 copy-start.8
  43.6 1.0 copy-start.9
  43.6 1.0 copy-start.12
  49.7 2.6 copy-start.13
  49.7 2.6 copy-start.14
  113.1 0.9 copy-start.10
  113.1 1.2 copy-start.11
  486.2 2.7 copy-start
  486.2 2.7 copy-start.7
Sparse Core Ops, SparseCore 0:
  113.3 116.7 all-gather.1
where the time goes:
time: 522 us; the launch traced here: 519 us
  local copies, waits for them, and re-layouts  149 us (29%)
  other arithmetic  121 us (23%)
  blocking collectives  100 us (19%)
  waiting for transfers between devices  81.8 us (16%)
  matrix products  43.7 us (8%)
  between operations  13.7 us (3%)
  starting transfers between devices  8.91 us (2%)
    all_gather x1, waiting for transfers between devices, per_device(): lax.all_gather(arrived, 'lon', axis=2, tiled=True)  81.8 us
    another operation x2, other arithmetic, modulated_sum(): jnp.stack([column_piece * cos_part[:, None, :], column_piece * sin_part[:...  60 us
    all_to_all x1, blocking collectives, per_device(): lax.all_to_all(picked.reshape(band_count, -1, channel_count, cols_dev), '...  50.3 us
    all_to_all x1, blocking collectives, per_device(): lax.all_to_all(filtered.reshape(band_count, -1, channel_count, cols_dev),...  50.2 us
    another operation x1, local copies, waits for them, and re-layouts, modulated_sum(): jnp.stack([column_piece * cos_part[:, None, :], column_piece * sin_part[:...  47.7 us
    dot_general x1, matrix products, modulated_sum(): jnp.dot(flattened, kernel, precision=HIGHEST_PRECISION, preferred_element...  43.7 us
    reshape x1, local copies, waits for them, and re-layouts, modulated_sum(): flattened = stacked.reshape(-1, piece_count)  35.2 us
    scatter x2, local copies, waits for them, and re-layouts, per_device(): advected.at[:, placement, :].set(returned.transpose(1, 0, 2), mode='drop')  23 us
  transfers between devices with their start and end apart: 5, of which 1 were waited for; matrix products, arithmetic and copies ran while one was open for 12% of the time, Pallas kernels for 0%

commit v1 on v0

--- a/solution.py
+++ b/solution.py
@@ -5,6 +5,19 @@
 from jax.sharding import PartitionSpec as P
 
 HIGHEST_PRECISION = lax.Precision.HIGHEST
+
+
+def ring_gather(shard, axis, dim):
+    peers, index, span = (lax.axis_size(axis), lax.axis_index(axis), shard.shape[dim])
+    right = [(i, (i + 1) % peers) for i in range(peers)]
+    out = jnp.zeros((*shard.shape[:dim], peers * span, *shard.shape[dim + 1 :]), shard.dtype)
+    current = shard
+    for step in range(peers):
+        source = (index - step) % peers
+        out = lax.dynamic_update_slice_in_dim(out, current, source * span, axis=dim)
+        if step < peers - 1:
+            current = lax.ppermute(current, axis, right)
+    return out
 
 
 def with_halo(cells, sides, width, closed):
@@ -135,9 +148,7 @@
     damping_rows = table_lookup(damping, incoming_global)
     targets = segment_index * cols_dev + jnp.arange(cols_dev, dtype=jnp.int32)
     initial = jnp.zeros((2,) + arrived.shape, jnp.float32)
-    running = modulated_sum(
-        initial, lax.all_gather(arrived, "lon", axis=2, tiled=True), cutoffs, targets, lon_count
-    )
+    running = modulated_sum(initial, ring_gather(arrived, "lon", 2), cutoffs, targets, lon_count)
     filtered = finish_filter(running, arrived, cutoffs, targets, damping_rows, lon_count)
     returned = lax.all_to_all(
         filtered.reshape(band_count, -1, channel_count, cols_dev),

time: 522 us -> 870 us (1.67)
  local copies, waits for them, and re-layouts: 149 us -> 451 us
  waiting for transfers between devices: 81.8 us -> 139 us
  between operations: 13.7 us -> 0.83 us
    dynamic_update_slice x0 -> x8, local copies, waits for them, and re-layouts: none -> 311 us  [ring_gather(): out = lax.dynamic_update_slice_in_dim(out, current, source * span, axis=dim)]
    ppermute x0 -> x7, waiting for transfers between devices: none -> 139 us  [ring_gather(): current = lax.ppermute(current, axis, right)]
    all_gather x1 -> x0, waiting for transfers between devices: 81.8 us -> none  [per_device(): lax.all_gather(arrived, 'lon', axis=2, tiled=True)]
    another operation x1 -> x0, local copies, waits for them, and re-layouts: 47.7 us -> none  [modulated_sum(): jnp.stack([column_piece * cos_part[:, None, :], column_piece * sin_part[:...]
    ppermute x0 -> x7, local copies, waits for them, and re-layouts: none -> 27 us  [ring_gather(): current = lax.ppermute(current, axis, right)]
    broadcast_in_dim x0 -> x1, local copies, waits for them, and re-layouts: none -> 8.97 us  [ring_gather(): jnp.zeros((*shard.shape[:dim], peers * span, *shard.shape[dim + 1:]), sha...]
  transfers between devices with their start and end apart: 5 -> 11, of which waited for: 1 -> 6; matrix products, arithmetic and copies ran while one was open for 12% -> 43% of each run, Pallas kernels for 0% -> 0%
where the time goes in v1:
time: 870 us; the launch traced here: 858 us
  local copies, waits for them, and re-layouts  451 us (52%)
  waiting for transfers between devices  139 us (16%)
  other arithmetic  120 us (14%)
  blocking collectives  94.6 us (11%)
  matrix products  43.7 us (5%)
  starting transfers between devices  9.08 us (1%)
    dynamic_update_slice x8, local copies, waits for them, and re-layouts, ring_gather(): out = lax.dynamic_update_slice_in_dim(out, current, source * span, axis=dim)  311 us
    ppermute x7, waiting for transfers between devices, ring_gather(): current = lax.ppermute(current, axis, right)  139 us
    another operation x2, other arithmetic, modulated_sum(): jnp.stack([column_piece * cos_part[:, None, :], column_piece * sin_part[:...  57.8 us
    all_to_all x1, blocking collectives, per_device(): lax.all_to_all(picked.reshape(band_count, -1, channel_count, cols_dev), '...  50.3 us
    all_to_all x1, blocking collectives, per_device(): lax.all_to_all(filtered.reshape(band_count, -1, channel_count, cols_dev),...  44.3 us
    dot_general x1, matrix products, modulated_sum(): jnp.dot(flattened, kernel, precision=HIGHEST_PRECISION, preferred_element...  43.7 us
    reshape x1, local copies, waits for them, and re-layouts, modulated_sum(): flattened = stacked.reshape(-1, piece_count)  35.2 us
    ppermute x7, local copies, waits for them, and re-layouts, ring_gather(): current = lax.ppermute(current, axis, right)  27 us
  transfers between devices with their start and end apart: 11, of which 6 were waited for; matrix products, arithmetic and copies ran while one was open for 43% of the time, Pallas kernels for 0%

profile of v1, /device:TPU:0, one launch (start us, length us, event | category | flops | bytes accessed | tf_op | source)
XLA Modules:
  0.0 858.2 jit_solution(7588310639317248430)
XLA Ops:
  3.2 4.9 collective-permute-start.3
  32.6 4.3 fusion.42
  38.0 5.1 fusion.21
  47.4 50.3 %all_to_all.10 = f32[4,60,5,360]{3,1,2,0:T(8,128)S(1)} all-to-all(f32[4,60,5,360]{3,1,2,0:T(8,128)S(1)} %copy.88), channel_id=1, replica_groups=mesh['lat'=4,'lon'=8] {'lat'}, dimensions={0} | all-to-all | bytes 3456000 | tf_op jit(solution)/shard_map/all_to_all | solution.py:133
  101.7 23.8 %collective-permute-done.4 = f32[240,5,360]{2,0,1:T(8,128)S(1)} collective-permute-done((f32[240,5,360]{2,0,1:T(8,128)}, f32[240,5,360]{2,0,1:T(8,128)S(1)}, u32[]{:S(2)}, u32[]{:S(2)}) %collective-permute-start.4) | collective-permute-done | bytes 1728032 | tf_op jit(solution)/shard_map/ppermute | solution.py:19
  126.9 23.6 %collective-permute-done.5 = f32[240,5,360]{2,0,1:T(8,128)S(1)} collective-permute-done((f32[240,5,360]{2,0,1:T(8,128)S(1)}, f32[240,5,360]{2,0,1:T(8,128)S(1)}, u32[]{:S(2)}, u32[]{:S(2)}) %collective-permute-start.5) | collective-permute-done | bytes 1728032 | tf_op jit(solution)/shard_map/ppermute | solution.py:19
  151.8 23.6 %collective-permute-done.6 = f32[240,5,360]{2,0,1:T(8,128)S(1)} collective-permute-done((f32[240,5,360]{2,0,1:T(8,128)S(1)}, f32[240,5,360]{2,0,1:T(8,128)S(1)}, u32[]{:S(2)}, u32[]{:S(2)}) %collective-permute-start.6) | collective-permute-done | bytes 1728032 | tf_op jit(solution)/shard_map/ppermute | solution.py:19
  176.7 23.6 %collective-permute-done.7 = f32[240,5,360]{2,0,1:T(8,128)S(1)} collective-permute-done((f32[240,5,360]{2,0,1:T(8,128)S(1)}, f32[240,5,360]{2,0,1:T(8,128)S(1)}, u32[]{:S(2)}, u32[]{:S(2)}) %collective-permute-start.7) | collective-permute-done | bytes 1728032 | tf_op jit(solution)/shard_map/ppermute | solution.py:19
  201.5 23.7 %collective-permute-done.8 = f32[240,5,360]{2,0,1:T(8,128)} collective-permute-done((f32[240,5,360]{2,0,1:T(8,128)S(1)}, f32[240,5,360]{2,0,1:T(8,128)}, u32[]{:S(2)}, u32[]{:S(2)}) %collective-permute-start.8) | collective-permute-done | bytes 1728032 | tf_op jit(solution)/shard_map/ppermute | solution.py:19
  228.5 20.7 %collective-permute-done.9 = f32[240,5,360]{2,0,1:T(8,128)} collective-permute-done((f32[240,5,360]{2,0,1:T(8,128)}, f32[240,5,360]{2,0,1:T(8,128)}, u32[]{:S(2)}, u32[]{:S(2)}) %collective-permute-start.9) | collective-permute-done | bytes 1728032 | tf_op jit(solution)/shard_map/ppermute | solution.py:19
  249.4 14.0 %fusion.30 = (f32[240,2880]{1,0:T(8,128)}, f32[240,2880]{1,0:T(8,128)}) fusion(s32[240]{0:T(256)S(1)} %multiply_add_fusion), kind=kLoop, calls=%fused_computation.45 | loop fusion | flops 6220800 | bytes 5530560 | tf_op jit(solution)/shard_map/cos | solution.py:43
  263.5 18.3 %fusion.66 = f32[2880,360]{1,0:T(8,128)} fusion(s32[360]{0:T(512)S(1)} %iota_add_fusion), kind=kLoop, calls=%fused_computation.12.clone.clone.1 | loop fusion | flops 14515200 | bytes 4148640 | tf_op jit(solution)/shard_map/dot_general | solution.py:64
  284.1 9.0 %broadcast_in_dim.130 = f32[240,5,2880]{2,1,0:T(8,128)} broadcast(f32[]{:T(128)} %constant.133.clone.1), dimensions={} | broadcast | bytes 13824004 | tf_op jit(solution)/shard_map/broadcast_in_dim | solution.py:13
  293.1 16.7 %dynamic_update_slice.24 = f32[240,5,2880]{2,1,0:T(8,128)} dynamic-update-slice(f32[240,5,2880]{2,1,0:T(8,128)} %broadcast_in_dim.130, f32[240,5,360]{2,1,0:T(8,128)} %copy.91, s32[]{:T(128)} %constant.139.clone.1, s32[]{:T(128)} %constant.139.clone.1, s32[]{:T(128)S(6)} %select_n.189) | dynamic-update-slice | bytes 3456004 | tf_op jit(solution)/shard_map/dynamic_update_slice | solution.py:17
  309.8 3.9 copy.92
  313.7 42.0 %dynamic_update_slice.25 = f32[240,5,2880]{2,1,0:T(8,128)} dynamic-update-slice(f32[240,5,2880]{2,1,0:T(8,128)} %dynamic_update_slice.24, f32[240,5,360]{2,1,0:T(8,128)} %copy.92, s32[]{:T(128)} %constant.139.clone.1, s32[]{:T(128)} %constant.139.clone.1, s32[]{:T(128)S(6)} %select_n.191) | dynamic-update-slice | bytes 3456004 | tf_op jit(solution)/shard_map/dynamic_update_slice | solution.py:17
  355.7 3.9 copy.93
  359.5 42.1 %dynamic_update_slice.26 = f32[240,5,2880]{2,1,0:T(8,128)} dynamic-update-slice(f32[240,5,2880]{2,1,0:T(8,128)} %dynamic_update_slice.25, f32[240,5,360]{2,1,0:T(8,128)} %copy.93, s32[]{:T(128)} %constant.139.clone.1, s32[]{:T(128)} %constant.139.clone.1, s32[]{:T(128)S(6)} %select_n.193) | dynamic-update-slice | bytes 3456004 | tf_op jit(solution)/shard_map/dynamic_update_slice | solution.py:17
  401.6 3.9 copy.94
  405.5 42.1 %dynamic_update_slice.27 = f32[240,5,2880]{2,1,0:T(8,128)} dynamic-update-slice(f32[240,5,2880]{2,1,0:T(8,128)} %dynamic_update_slice.26, f32[240,5,360]{2,1,0:T(8,128)} %copy.94, s32[]{:T(128)} %constant.139.clone.1, s32[]{:T(128)} %constant.139.clone.1, s32[]{:T(128)S(6)} %select_n.195) | dynamic-update-slice | bytes 3456004 | tf_op jit(solution)/shard_map/dynamic_update_slice | solution.py:17
  451.4 42.1 %dynamic_update_slice.28 = f32[240,5,2880]{2,1,0:T(8,128)} dynamic-update-slice(f32[240,5,2880]{2,1,0:T(8,128)} %dynamic_update_slice.27, f32[240,5,360]{2,1,0:T(8,128)} %copy.95, s32[]{:T(128)} %constant.139.clone.1, s32[]{:T(128)} %constant.139.clone.1, s32[]{:T(128)S(6)} %select_n.197) | dynamic-update-slice | bytes 3456004 | tf_op jit(solution)/shard_map/dynamic_update_slice | solution.py:17
  497.4 42.1 %dynamic_update_slice.29 = f32[240,5,2880]{2,1,0:T(8,128)} dynamic-update-slice(f32[240,5,2880]{2,1,0:T(8,128)} %dynamic_update_slice.28, f32[240,5,360]{2,1,0:T(8,128)} %copy.96, s32[]{:T(128)} %constant.139.clone.1, s32[]{:T(128)} %constant.139.clone.1, s32[]{:T(128)S(6)} %select_n.199) | dynamic-update-slice | bytes 3456004 | tf_op jit(solution)/shard_map/dynamic_update_slice | solution.py:17
  543.3 42.3 %dynamic_update_slice.30 = f32[240,5,2880]{2,1,0:T(8,128)} dynamic-update-slice(f32[240,5,2880]{2,1,0:T(8,128)} %dynamic_update_slice.29, f32[240,5,360]{2,1,0:T(8,128)} %copy.97, s32[]{:T(128)} %constant.139.clone.1, s32[]{:T(128)} %constant.139.clone.1, s32[]{:T(128)S(6)} %select_n.201) | dynamic-update-slice | bytes 3456004 | tf_op jit(solution)/shard_map/dynamic_update_slice | solution.py:17
  585.6 3.9 copy.98
  589.5 42.1 %dynamic_update_slice.31 = f32[240,5,2880]{2,1,0:T(8,128)} dynamic-update-slice(f32[240,5,2880]{2,1,0:T(8,128)} %dynamic_update_slice.30, f32[240,5,360]{2,1,0:T(8,128)} %copy.98, s32[]{:T(128)} %constant.139.clone.1, s32[]{:T(128)} %constant.139.clone.1, s32[]{:T(128)S(6)} %select_n.203) | dynamic-update-slice | bytes 3456004 | tf_op jit(solution)/shard_map/dynamic_update_slice | solution.py:17
  631.6 25.0 %multiply_bitcast_fusion.1 = (f32[1,240,5,2880]{3,2,1,0:T(8,128)}, f32[1,240,5,2880]{3,2,1,0:T(8,128)}) fusion(f32[240,5,2880]{2,1,0:T(8,128)} %dynamic_update_slice.31, f32[240,2880]{1,0:T(8,128)} %get-tuple-element.17, f32[240,2880]{1,0:T(8,128)} %get-tuple-element.18), kind=kLoop, calls=%fused_computation.4 | loop fusion | flops 6912000 | bytes 47001600 | tf_op jit(solution)/shard_map/stack | solution.py:61
  656.5 32.8 %pad_maximum_fusion = f32[2,240,5,2880]{3,2,1,0:T(8,128)} fusion(f32[1,240,5,2880]{3,2,1,0:T(8,128)} %get-tuple-element.8, f32[1,240,5,2880]{3,2,1,0:T(8,128)} %get-tuple-element.7), kind=kLoop, calls=%fused_computation.2 | loop fusion | flops 6912000 | bytes 55296000 | tf_op jit(solution)/shard_map/stack | solution.py:61
  689.3 35.2 %reshape.271 = f32[2400,2880]{1,0:T(8,128)} reshape(f32[2,240,5,2880]{3,2,1,0:T(8,128)} %pad_maximum_fusion) | data formatting | bytes 55296000 | tf_op jit(solution)/shard_map/reshape | solution.py:62
  724.5 43.7 %fusion.6 = f32[2400,360]{0,1:T(8,128)S(1)} fusion(f32[2400,2880]{1,0:T(8,128)} %reshape.271, f32[2880,360]{1,0:T(8,128)} %fusion.66), kind=kOutput, calls=%fused_computation.13 | convolution fusion | flops 29859840000 | bytes 35251200 | tf_op jit(solution)/shard_map/dot_general | solution.py:64
  782.4 5.0 fusion.13
  787.7 44.3 %all_to_all.11 = f32[4,60,5,360]{3,1,2,0:T(8,128)S(1)} all-to-all(f32[4,60,5,360]{3,1,2,0:T(8,128)S(1)} %copy.102), channel_id=1, replica_groups=mesh['lat'=4,'lon'=8] {'lat'}, dimensions={0} | all-to-all | bytes 3456000 | tf_op jit(solution)/shard_map/all_to_all | solution.py:153
  834.7 21.5 %scatter_fusion = f32[5,240,360]{2,0,1:T(8,128)S(1)} fusion(f32[5,240,360]{2,0,1:T(8,128)S(1)} %copy-done, s32[240]{0:T(256)S(1)} %bitcast.30, f32[240,5,360]{2,1,0:T(8,128)} %bitcast.28), kind=kCustom, calls=%fused_computation.1 | custom fusion | bytes 5184960 | tf_op jit(solution)/shard_map/scatter | solution.py:162
  (107 shorter events, 78.0 us)
Async XLA Ops:
  0.0 2.3 copy-start.6
  2.3 7.2 copy-start.1
  2.3 7.2 copy-start.2
  2.6 8.2 copy-start.4
  3.2 33.8 %collective-permute-start.3 = (f32[6,1,360]{2,0,1:T(8,128)}, f32[6,1,360]{2,0,1:T(8,128)S(1)}, u32[]{:S(2)}, u32[]{:S(2)}) collective-permute-start(f32[6,1,360]{2,0,1:T(8,128)} %get-tuple-element.12), channel_id=1, source_target_pairs={{0,8},{8,16},{16,24},{1,9},{9,17},{17,25},{2,10},{10,18},{18,26},{... | collective-permute-start | bytes 25928 | tf_op jit(solution)/shard_map/ppermute | solution.py:31
  8.2 29.7 %collective-permute-start.2 = (f32[6,1,360]{2,0,1:T(8,128)S(1)}, f32[6,1,360]{2,0,1:T(8,128)S(1)}, u32[]{:S(2)}, u32[]{:S(2)}) collective-permute-start(f32[6,1,360]{2,0,1:T(8,128)S(1)} %get-tuple-element.11), channel_id=1, source_target_pairs={{8,0},{16,8},{24,16},{9,1},{17,9},{25,17},{10,2},{18,10},{26,18},{... | collective-permute-start | bytes 25928 | tf_op jit(solution)/shard_map/ppermute | solution.py:33
  12.8 12.6 %collective-permute-start.1 = (f32[6,240,1]{1,2,0:T(1,128)}, f32[6,240,1]{1,2,0:T(1,128)}, u32[]{:S(2)}, u32[]{:S(2)}) collective-permute-start(f32[6,240,1]{1,2,0:T(1,128)} %copy.82), channel_id=1, source_target_pairs={{0,1},{1,2},{2,3},{3,4},{4,5},{5,6},{6,7},{7,0},{8,9},{9,10},{10,1... | collective-permute-start | bytes 17288 | tf_op jit(solution)/shard_map/ppermute | solution.py:31
  14.2 16.6 %collective-permute-start = (f32[6,240,1]{1,2,0:T(1,128)S(1)}, f32[6,240,1]{1,2,0:T(1,128)}, u32[]{:S(2)}, u32[]{:S(2)}) collective-permute-start(f32[6,240,1]{1,2,0:T(1,128)S(1)} %copy.80), channel_id=1, source_target_pairs={{1,0},{2,1},{3,2},{4,3},{5,4},{6,5},{7,6},{0,7},{9,8},{10,9},{11,1... | collective-permute-start | bytes 17288 | tf_op jit(solution)/shard_map/ppermute | solution.py:33
  32.6 4.4 copy-start.5
  37.0 1.0 copy-start.7
  37.0 1.0 copy-start.13
  37.0 1.0 copy-start.14
  37.0 1.0 copy-start.17
  43.0 2.6 copy-start.18
  43.1 2.6 copy-start.19
  99.1 127.0 %copy-start.15 = (s32[960]{0:T(1024)S(1)}, s32[960]{0:T(1024)}, u32[]{:S(2)}) copy-start(s32[960]{0:T(1024)} %param.9) | copy-start | bytes 11524
  99.1 127.4 %copy-start.16 = (f32[960]{0:T(1024)S(1)}, f32[960]{0:T(1024)}, u32[]{:S(2)}) copy-start(f32[960]{0:T(1024)} %param.10) | copy-start | bytes 11524
  101.7 23.8 %collective-permute-start.4 = (f32[240,5,360]{2,0,1:T(8,128)}, f32[240,5,360]{2,0,1:T(8,128)S(1)}, u32[]{:S(2)}, u32[]{:S(2)}) collective-permute-start(f32[240,5,360]{2,0,1:T(8,128)} %reshape.270), channel_id=1, source_target_pairs={{0,1},{1,2},{2,3},{3,4},{4,5},{5,6},{6,7},{7,0},{8,9},{9,10},{10,1... | collective-permute-start | bytes 5184008 | tf_op jit(solution)/shard_map/ppermute | solution.py:19
  125.6 1.3 copy-start.8
  126.9 23.6 %collective-permute-start.5 = (f32[240,5,360]{2,0,1:T(8,128)S(1)}, f32[240,5,360]{2,0,1:T(8,128)S(1)}, u32[]{:S(2)}, u32[]{:S(2)}) collective-permute-start(f32[240,5,360]{2,0,1:T(8,128)S(1)} %collective-permute-done.4), channel_id=1, source_target_pairs={{0,1},{1,2},{2,3},{3,4},{4,5},{5,6},{6,7},{7,0},{8,9},{9,10},{10,1... | collective-permute-start | bytes 5184008 | tf_op jit(solution)/shard_map/ppermute | solution.py:19
  150.5 1.3 copy-start.9
  151.8 23.6 %collective-permute-start.6 = (f32[240,5,360]{2,0,1:T(8,128)S(1)}, f32[240,5,360]{2,0,1:T(8,128)S(1)}, u32[]{:S(2)}, u32[]{:S(2)}) collective-permute-start(f32[240,5,360]{2,0,1:T(8,128)S(1)} %collective-permute-done.5), channel_id=1, source_target_pairs={{0,1},{1,2},{2,3},{3,4},{4,5},{5,6},{6,7},{7,0},{8,9},{9,10},{10,1... | collective-permute-start | bytes 5184008 | tf_op jit(solution)/shard_map/ppermute | solution.py:19
  175.4 1.2 copy-start.10
  176.7 23.6 %collective-permute-start.7 = (f32[240,5,360]{2,0,1:T(8,128)S(1)}, f32[240,5,360]{2,0,1:T(8,128)S(1)}, u32[]{:S(2)}, u32[]{:S(2)}) collective-permute-start(f32[240,5,360]{2,0,1:T(8,128)S(1)} %collective-permute-done.6), channel_id=1, source_target_pairs={{0,1},{1,2},{2,3},{3,4},{4,5},{5,6},{6,7},{7,0},{8,9},{9,10},{10,1... | collective-permute-start | bytes 5184008 | tf_op jit(solution)/shard_map/ppermute | solution.py:19
  200.3 1.2 copy-start.11
  201.5 23.7 %collective-permute-start.8 = (f32[240,5,360]{2,0,1:T(8,128)S(1)}, f32[240,5,360]{2,0,1:T(8,128)}, u32[]{:S(2)}, u32[]{:S(2)}) collective-permute-start(f32[240,5,360]{2,0,1:T(8,128)S(1)} %collective-permute-done.7), channel_id=1, source_target_pairs={{0,1},{1,2},{2,3},{3,4},{4,5},{5,6},{6,7},{7,0},{8,9},{9,10},{10,1... | collective-permute-start | bytes 5184008 | tf_op jit(solution)/shard_map/ppermute | solution.py:19
  225.3 24.0 %collective-permute-start.9 = (f32[240,5,360]{2,0,1:T(8,128)}, f32[240,5,360]{2,0,1:T(8,128)}, u32[]{:S(2)}, u32[]{:S(2)}) collective-permute-start(f32[240,5,360]{2,0,1:T(8,128)} %collective-permute-done.8), channel_id=1, source_target_pairs={{0,1},{1,2},{2,3},{3,4},{4,5},{5,6},{6,7},{7,0},{8,9},{9,10},{10,1... | collective-permute-start | bytes 5184008 | tf_op jit(solution)/shard_map/ppermute | solution.py:19
  249.2 336.4 %collective-permute-start.10 = (f32[240,5,360]{2,0,1:T(8,128)}, f32[240,5,360]{2,0,1:T(8,128)}, u32[]{:S(2)}, u32[]{:S(2)}) collective-permute-start(f32[240,5,360]{2,0,1:T(8,128)} %collective-permute-done.9), channel_id=1, source_target_pairs={{0,1},{1,2},{2,3},{3,4},{4,5},{5,6},{6,7},{7,0},{8,9},{9,10},{10,1... | collective-permute-start | bytes 5184008 | tf_op jit(solution)/shard_map/ppermute | solution.py:19
  263.5 18.3 %copy-start.3 = (f32[240,5,360]{2,0,1:T(8,128)S(1)}, f32[240,5,360]{2,0,1:T(8,128)}, u32[]{:S(2)}) copy-start(f32[240,5,360]{2,0,1:T(8,128)} %reshape.270) | copy-start | bytes 5184004
  832.0 2.7 copy-start
  832.0 2.7 copy-start.12
